TPU v7x, 32 devices: a whole 2x2x4 slice. The times are simulated.
32 devices in a mesh: ctx: 8 (over y, x, core), fsdp: 4 (over z).
Axes of the slice: x: 2, y: 2, z: 4, core: 2. Of those that a mesh axis runs over, the one named last changes fastest.
Arguments:
- tokens: bfloat16 [4, 4096, 2048], P('fsdp', 'ctx'), may hold values from -6 to 6
- cotangent: bfloat16 [4, 4096, 2048], P('fsdp', 'ctx'), may hold values from -6 to 6
- kv_cotangent: bfloat16 [4, 4096, 256], P('fsdp', 'ctx'), may hold values from -6 to 6
- lengths: int32 [4], P('fsdp'), may hold values from 1024 to 4096, as said below
- block_order: int32 [4, 16], P('fsdp'), may hold values from 0 to 15, each once within a row
- w_query: bfloat16 [2048, 2048], P('fsdp'), may hold values from -0.125 to 0.125
- w_kv: bfloat16 [2048, 256], P('fsdp'), may hold values from -0.25 to 0.25
- w_out: bfloat16 [2048, 2048], P('fsdp'), may hold values from -0.375 to 0.375
- gain_attn: bfloat16 [2048], P('fsdp'), may hold values from 0.5 to 1.5
- gain_ffn: bfloat16 [2048], P('fsdp'), may hold values from 0.5 to 1.5
- w_gate: bfloat16 [2048, 5632], P(None, 'fsdp'), may hold values from -0.125 to 0.125
- w_up: bfloat16 [2048, 5632], P(None, 'fsdp'), may hold values from -0.125 to 0.125
- w_down: bfloat16 [2048, 5632], P(None, 'fsdp'), may hold values from -0.078125 to 0.078125
Outputs:
- output: bfloat16 [4, 4096, 2048], P('fsdp', 'ctx')
- input_grad: bfloat16 [4, 4096, 2048], P('fsdp', 'ctx')
- grad_w_query: float32 [2048, 2048], P(('ctx', 'fsdp'))
- grad_w_kv: float32 [2048, 256], P(('ctx', 'fsdp'))
- grad_w_out: float32 [2048, 2048], P(('ctx', 'fsdp'))
- grad_gain_attn: float32 [2048], P(('ctx', 'fsdp'))
- grad_gain_ffn: float32 [2048], P(('ctx', 'fsdp'))
- grad_w_gate: float32 [2048, 5632], P('ctx', 'fsdp')
- grad_w_up: float32 [2048, 5632], P('ctx', 'fsdp')
- grad_w_down: float32 [2048, 5632], P('ctx', 'fsdp')
Inputs may be any that keep to these rules, and one draw needn't show every extreme that they name: Slot s holds one sequence of lengths[s] tokens; in every draw some slot is full. Each row is a permutation: stored block j of slot s, its tokens j * 256 to (j + 1) * 256 - 1, holds positions block_order[s, j] * 256 onward.
All inputs are finite; a program needn't handle non-finite values.
Results may differ from a plain program's by a relative error of at most 0.025.
Values may be sent and summed in bfloat16 or wider, within the bound.
No kernel may reach another device: no remote copies, remote signals or barrier semaphores. Data moves between devices by JAX's collectives and lax.ppermute only.
A program may use at most 448 MiB of HBM per device.

v0:
```python
import jax
import jax.numpy as jnp
from jax import lax
from jax.sharding import PartitionSpec as P

H = 16
HD = 128
EPSILON = 1e-05
ROPE_BASE = 10000.0
MASKED = -1e30


def angles(positions, head_dim):
    half_dim = head_dim // 2
    frequency = ROPE_BASE ** (-2.0 * jnp.arange(half_dim, dtype=jnp.float32) / head_dim)
    phase_angle = positions.astype(jnp.float32)[:, None] * frequency[None, :]
    return (jnp.cos(phase_angle), jnp.sin(phase_angle))


def rotate(vectors, cosine, sine_vals):
    half_dim = cosine.shape[-1]
    first_half = vectors[..., :half_dim]
    second_half = vectors[..., half_dim:]
    return jnp.concatenate(
        [
            first_half * cosine - second_half * sine_vals,
            second_half * cosine + first_half * sine_vals,
        ],
        axis=-1,
    )


def contract_rows(left, right):
    return lax.dot_general(
        left, right, (((0,), (0,)), ((), ())), preferred_element_type=jnp.float32
    )


def contract_cols(left, right):
    return lax.dot_general(
        left, right, (((1,), (1,)), ((), ())), preferred_element_type=jnp.float32
    )


def score_block(query_rows, row_pos, keys_all, key_pos, length, offset_at, block_width):
    key_part = lax.dynamic_slice_in_dim(keys_all, offset_at, block_width, 0)
    pos_part = lax.dynamic_slice_in_dim(key_pos, offset_at, block_width, 0)
    scores = contract_cols(query_rows, key_part)
    allowed = (pos_part[None, :] <= row_pos[:, None]) & (pos_part[None, :] < length)
    return jnp.where(allowed, scores, MASKED)


def attention_forward(query_rot, kv_slot, query_pos, key_pos, length):
    local_len, head_count, head_dim = query_rot.shape
    rows_total = local_len * head_count
    query_rows = query_rot.reshape(rows_total, head_dim)
    row_pos = jnp.repeat(query_pos, head_count)
    keys_all = kv_slot[:, :head_dim]
    values_all = kv_slot[:, head_dim:]
    block_width = min(512, kv_slot.shape[0])
    steps_count = kv_slot.shape[0] // block_width

    def stat_update(carried, offset_at):
        maximum, running_sum = carried
        scores = score_block(query_rows, row_pos, keys_all, key_pos, length, offset_at, block_width)
        new_max = jnp.maximum(maximum, jnp.max(scores, axis=1))
        summed = running_sum * jnp.exp(maximum - new_max) + jnp.sum(
            jnp.exp(scores - new_max[:, None]), axis=1
        )
        return (new_max, summed)

    def stat_step(carried, step_index):
        offset_at = step_index * block_width
        carried = stat_update(carried, offset_at)
        return (carried, None)

    initial = (jnp.full((rows_total,), MASKED, jnp.float32), jnp.zeros((rows_total,), jnp.float32))
    (maximum, running_sum), unused = lax.scan(
        stat_step, initial, jnp.arange(steps_count, dtype=jnp.int32)
    )
    log_total = maximum + jnp.log(running_sum)

    def value_update(accumulated, offset_at):
        scores = score_block(query_rows, row_pos, keys_all, key_pos, length, offset_at, block_width)
        weights_low = jnp.exp(scores - log_total[:, None]).astype(jnp.bfloat16)
        value_part = lax.dynamic_slice_in_dim(values_all, offset_at, block_width, 0)
        return accumulated + jnp.dot(weights_low, value_part, preferred_element_type=jnp.float32)

    def value_step(accumulated, step_index):
        offset_at = step_index * block_width
        accumulated = value_update(accumulated, offset_at)
        return (accumulated, None)

    attention, unused = lax.scan(
        value_step,
        jnp.zeros((rows_total, head_dim), jnp.float32),
        jnp.arange(steps_count, dtype=jnp.int32),
    )
    return (attention.reshape(local_len, head_count * head_dim), log_total)


def attention_backward(
    query_rot, kv_slot, query_pos, key_pos, length, log_total, grad_attn, row_delta
):
    local_len, head_count, head_dim = query_rot.shape
    rows_total = local_len * head_count
    query_rows = query_rot.reshape(rows_total, head_dim)
    grad_rows = grad_attn.reshape(rows_total, head_dim)
    row_pos = jnp.repeat(query_pos, head_count)
    keys_all = kv_slot[:, :head_dim]
    values_all = kv_slot[:, head_dim:]
    block_width = min(512, kv_slot.shape[0])
    steps_count = kv_slot.shape[0] // block_width

    def grad_update(grad_query, offset_at):
        scores = score_block(query_rows, row_pos, keys_all, key_pos, length, offset_at, block_width)
        probability = jnp.exp(scores - log_total[:, None])
        key_part = lax.dynamic_slice_in_dim(keys_all, offset_at, block_width, 0)
        value_part = lax.dynamic_slice_in_dim(values_all, offset_at, block_width, 0)
        grad_prob = contract_cols(grad_rows, value_part)
        grad_score = (probability * (grad_prob - row_delta[:, None])).astype(jnp.bfloat16)
        grad_key = contract_rows(grad_score, query_rows)
        grad_value = contract_rows(probability.astype(jnp.bfloat16), grad_rows)
        updated = grad_query + jnp.dot(grad_score, key_part, preferred_element_type=jnp.float32)
        return (updated, jnp.concatenate([grad_key, grad_value], axis=1))

    def grad_step(grad_query, step_index):
        offset_at = step_index * block_width
        return grad_update(grad_query, offset_at)

    grad_query, key_grads = lax.scan(
        grad_step,
        jnp.zeros((rows_total, head_dim), jnp.float32),
        jnp.arange(steps_count, dtype=jnp.int32),
    )
    return (
        grad_query.reshape(local_len, head_count, head_dim),
        key_grads.reshape(steps_count * block_width, 2 * head_dim),
    )


def swiglu_back(gate_proj, up_proj, grad_hidden):
    sigmoid_gate = jax.nn.sigmoid(gate_proj)
    grad_float = grad_hidden.astype(jnp.float32)
    grad_gate = (
        grad_float * up_proj * sigmoid_gate * (1.0 + gate_proj * (1.0 - sigmoid_gate))
    ).astype(jnp.bfloat16)
    grad_up = (grad_float * (gate_proj * sigmoid_gate)).astype(jnp.bfloat16)
    return (grad_gate, grad_up)


def split_term(left, right, ctx_count, fsdp_count):
    left_split = left.reshape(left.shape[0], ctx_count, left.shape[1] // ctx_count)
    right_split = right.reshape(right.shape[0], fsdp_count, right.shape[1] // fsdp_count)
    grad_term = jnp.einsum(
        "tcd,tfk->cfdk", left_split, right_split, preferred_element_type=jnp.float32
    )
    return grad_term.reshape(ctx_count * fsdp_count * grad_term.shape[2], grad_term.shape[3])


def shards(
    tokens,
    cotangent,
    kv_cotangent,
    lengths,
    block_order,
    w_query,
    w_kv,
    w_out,
    gain_attn,
    gain_ffn,
    w_gate,
    w_up,
    w_down,
):
    slots_here, local_len, model_dim = tokens.shape
    ctx_count = lax.axis_size("ctx")
    fsdp_count = lax.axis_size("fsdp")
    head_dim = HD
    head_count = H
    block_len = local_len // 2
    slot_len = local_len * ctx_count
    local_rows = slots_here * local_len
    offsets = jnp.arange(slot_len, dtype=jnp.int32) % block_len
    key_pos = jnp.repeat(block_order, block_len, axis=1) * block_len + offsets[None, :]
    query_pos = lax.dynamic_slice_in_dim(key_pos, lax.axis_index("ctx") * local_len, local_len, 1)
    live_rows = (query_pos < lengths[:, None]).reshape(local_rows, 1)
    query_full, kv_full, out_full, gain_one, gain_two = (
        lax.all_gather(w_query, "fsdp", axis=0, tiled=True),
        lax.all_gather(w_kv, "fsdp", axis=0, tiled=True),
        lax.all_gather(w_out, "fsdp", axis=0, tiled=True),
        lax.all_gather(gain_attn, "fsdp", axis=0, tiled=True),
        lax.all_gather(gain_ffn, "fsdp", axis=0, tiled=True),
    )
    tokens_flat = tokens.reshape(local_rows, model_dim).astype(jnp.float32)
    inverse_one = lax.rsqrt(jnp.mean(tokens_flat * tokens_flat, axis=1, keepdims=True) + EPSILON)
    unit_one = tokens_flat * inverse_one
    normed_attn = (unit_one * gain_one.astype(jnp.float32)).astype(jnp.bfloat16)
    queries = jnp.dot(normed_attn, query_full, preferred_element_type=jnp.float32).reshape(
        local_rows, head_count, head_dim
    )
    key_value = jnp.dot(normed_attn, kv_full, preferred_element_type=jnp.float32)
    cosine, sine_vals = angles(query_pos.reshape(local_rows), head_dim)
    query_rot = (
        rotate(queries, cosine[:, None, :], sine_vals[:, None, :]) * head_dim ** (-0.5)
    ).astype(jnp.bfloat16)
    key_rot = rotate(key_value[:, :head_dim], cosine, sine_vals).astype(jnp.bfloat16)
    local_kv = jnp.concatenate([key_rot, key_value[:, head_dim:].astype(jnp.bfloat16)], axis=1)
    slot_kv = lax.all_gather(
        local_kv.reshape(slots_here, local_len, 2 * head_dim), "ctx", axis=1, tiled=True
    )
    slot_queries = query_rot.reshape(slots_here, local_len, head_count, head_dim)

    def slot_forward(inputs):
        query_slot, kv_slot, pos_query, pos_key, length, order_row = inputs
        return attention_forward(query_slot, kv_slot, pos_query, pos_key, length)

    attention, log_total = lax.map(
        slot_forward, (slot_queries, slot_kv, query_pos, key_pos, lengths, block_order)
    )
    attention = attention.reshape(local_rows, head_count * head_dim)
    attn_low = attention.astype(jnp.bfloat16)
    residual = tokens_flat + jnp.dot(attn_low, out_full, preferred_element_type=jnp.float32)
    inverse_two = lax.rsqrt(jnp.mean(residual * residual, axis=1, keepdims=True) + EPSILON)
    unit_two = residual * inverse_two
    normed_ffn = (unit_two * gain_two.astype(jnp.float32)).astype(jnp.bfloat16)
    grad_out = jnp.where(
        live_rows, cotangent.reshape(local_rows, model_dim), jnp.zeros((), jnp.bfloat16)
    )
    gate_full, up_full, down_full = (
        lax.all_gather(w_gate, "fsdp", axis=1, tiled=True),
        lax.all_gather(w_up, "fsdp", axis=1, tiled=True),
        lax.all_gather(w_down, "fsdp", axis=1, tiled=True),
    )
    gate_proj = jnp.dot(normed_ffn, gate_full, preferred_element_type=jnp.float32)
    up_proj = jnp.dot(normed_ffn, up_full, preferred_element_type=jnp.float32)
    hidden = (jax.nn.silu(gate_proj) * up_proj).astype(jnp.bfloat16)
    ffn_out = contract_cols(hidden, down_full)
    grad_hidden = jnp.dot(grad_out, down_full, preferred_element_type=jnp.float32).astype(
        jnp.bfloat16
    )
    grad_gate, grad_up = swiglu_back(gate_proj, up_proj, grad_hidden)
    grad_normed = contract_cols(grad_gate, gate_full) + contract_cols(grad_up, up_full)
    ffn_grads = (
        lax.psum_scatter(
            split_term(normed_ffn, grad_gate, ctx_count, fsdp_count),
            ("ctx", "fsdp"),
            scatter_dimension=0,
            tiled=True,
        ),
        lax.psum_scatter(
            split_term(normed_ffn, grad_up, ctx_count, fsdp_count),
            ("ctx", "fsdp"),
            scatter_dimension=0,
            tiled=True,
        ),
        lax.psum_scatter(
            split_term(grad_out, hidden, ctx_count, fsdp_count),
            ("ctx", "fsdp"),
            scatter_dimension=0,
            tiled=True,
        ),
    )
    output = jnp.where(live_rows, residual + ffn_out, 0.0)
    grad_gain_two = jnp.sum(grad_normed * unit_two, axis=0)
    scaled_two = grad_normed * gain_two.astype(jnp.float32)
    grad_residual = grad_out.astype(jnp.float32) + inverse_two * (
        scaled_two - unit_two * jnp.mean(scaled_two * unit_two, axis=1, keepdims=True)
    )
    grad_branch = grad_residual.astype(jnp.bfloat16)
    grad_attn = contract_cols(grad_branch, out_full).astype(jnp.bfloat16)
    row_delta = jnp.sum(
        grad_attn.astype(jnp.float32).reshape(local_rows, head_count, head_dim)
        * attention.reshape(local_rows, head_count, head_dim),
        axis=2,
    )

    def slot_backward(inputs):
        (
            query_slot,
            kv_slot,
            pos_query,
            pos_key,
            length,
            log_slot,
            grad_slot,
            delta_slot,
            order_row,
        ) = inputs
        grad_query_slot, key_grads = attention_backward(
            query_slot, kv_slot, pos_query, pos_key, length, log_slot, grad_slot, delta_slot
        )
        return (grad_query_slot, key_grads)

    grad_query_rot, key_terms = lax.map(
        slot_backward,
        (
            slot_queries,
            slot_kv,
            query_pos,
            key_pos,
            lengths,
            log_total,
            grad_attn.reshape(slots_here, local_len, head_count, head_dim),
            row_delta.reshape(slots_here, local_len * head_count),
            block_order,
        ),
    )
    key_sums = lax.psum_scatter(
        key_terms.astype(jnp.bfloat16), "ctx", scatter_dimension=1, tiled=True
    ).astype(jnp.float32)
    kv_total = key_sums + jnp.where(
        live_rows.reshape(slots_here, local_len, 1), kv_cotangent.astype(jnp.float32), 0.0
    )
    grad_kv_low = kv_total.reshape(local_rows, 2 * head_dim).astype(jnp.bfloat16)
    grad_key = rotate(grad_kv_low[:, :head_dim].astype(jnp.float32), cosine, -sine_vals)
    grad_kv = jnp.concatenate(
        [grad_key, grad_kv_low[:, head_dim:].astype(jnp.float32)], axis=1
    ).astype(jnp.bfloat16)
    grad_qrot = (
        grad_query_rot.reshape(local_rows, head_count, head_dim)
        .astype(jnp.bfloat16)
        .astype(jnp.float32)
    )
    grad_query = (
        (rotate(grad_qrot, cosine[:, None, :], -sine_vals[:, None, :]) * head_dim ** (-0.5))
        .reshape(local_rows, head_count * head_dim)
        .astype(jnp.bfloat16)
    )
    grad_normed_one = contract_cols(grad_query, query_full) + contract_cols(grad_kv, kv_full)
    grad_gain_one = jnp.sum(grad_normed_one * unit_one, axis=0)
    scaled_one = grad_normed_one * gain_one.astype(jnp.float32)
    grad_tokens = grad_residual + inverse_one * (
        scaled_one - unit_one * jnp.mean(scaled_one * unit_one, axis=1, keepdims=True)
    )
    attn_grads = (
        lax.psum_scatter(
            contract_rows(normed_attn, grad_query), ("ctx", "fsdp"), scatter_dimension=0, tiled=True
        ),
        lax.psum_scatter(
            contract_rows(normed_attn, grad_kv), ("ctx", "fsdp"), scatter_dimension=0, tiled=True
        ),
        lax.psum_scatter(
            contract_rows(attn_low, grad_branch), ("ctx", "fsdp"), scatter_dimension=0, tiled=True
        ),
        lax.psum_scatter(grad_gain_one, ("ctx", "fsdp"), scatter_dimension=0, tiled=True),
        lax.psum_scatter(grad_gain_two, ("ctx", "fsdp"), scatter_dimension=0, tiled=True),
    )
    return (
        output.reshape(tokens.shape).astype(jnp.bfloat16),
        grad_tokens.reshape(tokens.shape).astype(jnp.bfloat16),
        attn_grads[0],
        attn_grads[1],
        attn_grads[2],
        attn_grads[3],
        attn_grads[4],
        ffn_grads[0],
        ffn_grads[1],
        ffn_grads[2],
    )


def solution(mesh):
    return jax.shard_map(
        shards,
        mesh=mesh,
        in_specs=(
            P("fsdp", "ctx", None),
            P("fsdp", "ctx", None),
            P("fsdp", "ctx", None),
            P("fsdp"),
            P("fsdp", None),
            P("fsdp", None),
            P("fsdp", None),
            P("fsdp", None),
            P("fsdp"),
            P("fsdp"),
            P(None, "fsdp"),
            P(None, "fsdp"),
            P(None, "fsdp"),
        ),
        out_specs=(
            P("fsdp", "ctx", None),
            P("fsdp", "ctx", None),
            P(("ctx", "fsdp"), None),
            P(("ctx", "fsdp"), None),
            P(("ctx", "fsdp"), None),
            P(("ctx", "fsdp")),
            P(("ctx", "fsdp")),
            P("ctx", "fsdp"),
            P("ctx", "fsdp"),
            P("ctx", "fsdp"),
        ),
        check_vma=False,
    )
```

profile of v0, /device:TPU:0, one launch (start us, length us, event | category | flops | bytes accessed | tf_op | source)
XLA Modules:
  0.0 5840.0 jit_solution(3675595155620998251)
XLA Ops:
  8.6 13.5 all-gather.1
  26.3 14.0 all-gather.11.cloned.1.call-done
  47.8 12.2 all-gather.2
  60.0 12.3 all-gather.23.cloned.1.call-done
  75.9 147.6 %all-gather.13.cloned.1.call-done = bf16[2048,2048]{1,0:T(8,128)(2,1)} async-done(((bf16[512,2048]{1,0:T(8,128)(2,1)}), bf16[2048,2048]{1,0:T(8,128)(2,1)}) %all-gather.13.cloned.1.call-update) | async-done | bytes 8388624 | tf_op jit(solution)/shard_map/all_gather | solution.py:189
  223.5 12.6 copy.58
  258.7 154.5 %while.58 = (s32[]{:T(128)}, f32[8192]{0:T(1024)S(1)}, f32[8192]{0:T(1024)S(1)}, s32[8]{0:T(128)S(1)}, s32[4096]{0:T(1024)S(1)}, /*index=5*/s32[]{:T(128)}, bf16...) while((s32[]{:T(128)}, f32[8192]{0:T(1024)S(1)}, ...), condition=%wide.region_4.5_spmd.clone, body=%wide.region_1.4_spmd.clone.sunk | while | flops 1111532032 | bytes 36384468 | solution.py:78
  413.8 110.5 %while.59 = (s32[]{:T(128)}, f32[8192,128]{1,0:T(8,128)}, s32[8]{0:T(128)S(1)}, s32[4096]{0:T(1024)S(1)}, s32[]{:T(128)}, /*index=5*/bf16[4096,128]{1,0:T(8,128)...) while((s32[]{:T(128)}, f32[8192,128]{1,0:T(8,128)}, ...), condition=%wide.region_6.7_spmd.clone, body=%wide.region_5.6_spmd.clone.sunk | while | flops 2170552832 | bytes 10922712 | solution.py:94
  546.5 217.1 %all-gather.17.cloned.1.call-done = bf16[2048,5632]{1,0:T(8,128)(2,1)} async-done(((bf16[2048,1408]{1,0:T(8,128)(2,1)}), bf16[2048,5632]{1,0:T(8,128)(2,1)}) %all-gather.17.cloned.1.call-update) | async-done | bytes 23068688 | tf_op jit(solution)/shard_map/all_gather | solution.py:231
  763.6 19.9 fusion.102
  783.5 371.0 %all-gather.21.cloned.1.call-done = bf16[2048,5632]{1,0:T(8,128)(2,1)} async-done(((bf16[2048,1408]{1,0:T(8,128)(2,1)}), bf16[2048,5632]{1,0:T(8,128)(2,1)}) %all-gather.21.cloned.1.call-update) | async-done | bytes 23068688 | tf_op jit(solution)/shard_map/all_gather | solution.py:233
  1154.5 18.4 convolution_convert_fusion
  1172.9 372.6 %all-gather.19.cloned.1.call-done = bf16[2048,5632]{1,0:T(8,128)(2,1)} async-done(((bf16[2048,1408]{1,0:T(8,128)(2,1)}), bf16[2048,5632]{1,0:T(8,128)(2,1)}) %all-gather.19.cloned.1.call-update) | async-done | bytes 23068688 | tf_op jit(solution)/shard_map/all_gather | solution.py:232
  1545.5 27.0 fusion.34
  1572.6 19.5 fusion.103
  1592.1 19.4 multiply_reduce_fusion
  1632.9 354.3 %while.60 = (s32[]{:T(128)}, f32[8192,128]{1,0:T(8,128)}, bf16[8,512,256]{1,2,0:T(8,128)(2,1)}, s32[8]{0:T(128)S(1)}, s32[4096]{0:T(1024)}, /*index=5*/s32[]{:T(...) while((s32[]{:T(128)}, f32[8192,128]{1,0:T(8,128)}, ...), condition=%wide.region_11.12_spmd.clone, body=%wide.region_10.11_spmd.clone.sunk | while | flops 5404885504 | bytes 127214928 | solution.py:131
  1996.4 39.1 reduce-scatter.8.cloned.1.call-done
  2039.7 13.2 fusion.65
  2095.6 20.8 convolution_bitcast_fusion.2
  2116.4 33.3 copy.72
  2161.0 20.9 convolution_bitcast_fusion.1
  2181.9 33.5 copy.75
  2232.5 20.8 convolution_bitcast_fusion
  2253.3 33.3 copy.78
  2286.6 19.9 fusion.59
  2318.5 42.5 all-reduce.2
  2368.1 175.8 %reduce-scatter.14.cloned.1.call-done = f32[64,2048]{1,0:T(8,128)} async-done(((f32[2048,2048]{1,0:T(8,128)}), f32[64,2048]{1,0:T(8,128)}) %reduce-scatter.14.cloned.1.call-update) | async-done | bytes 524304 | tf_op jit(solution)/shard_map/reduce_scatter | solution.py:343
  2543.9 365.1 %reduce-scatter.10.cloned.1.call-done = f32[64,2048]{1,0:T(8,128)} async-done(((f32[2048,2048]{1,0:T(8,128)}), f32[64,2048]{1,0:T(8,128)}) %reduce-scatter.10.cloned.1.call-update) | async-done | bytes 524304 | tf_op jit(solution)/shard_map/reduce_scatter | solution.py:337
  2909.0 973.1 %reduce-scatter.16.cloned.1.call-done = f32[256,1408]{1,0:T(8,128)} async-done(((f32[8192,1408]{1,0:T(8,128)}), f32[256,1408]{1,0:T(8,128)}) %reduce-scatter.16.cloned.1.call-update) | async-done | bytes 1441808 | tf_op jit(solution)/shard_map/reduce_scatter | solution.py:245
  3882.1 975.7 %reduce-scatter.18.cloned.1.call-done = f32[256,1408]{1,0:T(8,128)} async-done(((f32[8192,1408]{1,0:T(8,128)}), f32[256,1408]{1,0:T(8,128)}) %reduce-scatter.18.cloned.1.call-update) | async-done | bytes 1441808 | tf_op jit(solution)/shard_map/reduce_scatter | solution.py:251
  4857.7 975.5 %reduce-scatter.20.cloned.1.call-done = f32[256,1408]{1,0:T(8,128)} async-done(((f32[8192,1408]{1,0:T(8,128)}), f32[256,1408]{1,0:T(8,128)}) %reduce-scatter.20.cloned.1.call-update) | async-done | bytes 1441808 | tf_op jit(solution)/shard_map/reduce_scatter | solution.py:257
  (438 shorter events, 787.4 us)
Async XLA Ops:
  7.2 33.1 all-gather.11.cloned.1.call-start
  7.9 64.3 %all-gather.23.cloned.1.call-start = ((), (), s32[]{:S(2)}) async-start(), calls=%async_computation.20 | async-start | bytes 2359296 | tf_op jit(solution)/shard_map/all_gather | solution.py:209
  22.2 213.9 %copy-start.28 = (f32[4,1,512]{2,1,0:T(1,128)}, f32[4,1,512]{2,1,0:T(1,128)S(1)}, u32[]{:S(2)}) copy-start(f32[4,1,512]{2,1,0:T(1,128)S(1)} %convert_element_type.188) | copy-start | bytes 24580
  24.2 20.2 copy-start.32
  24.2 20.2 copy-start.41
  26.3 209.9 %copy-start.34 = (f32[512]{0:T(512)}, f32[512]{0:T(512)S(1)}, u32[]{:S(2)}) copy-start(f32[512]{0:T(512)S(1)} %add_rsqrt_fusion.1) | copy-start | bytes 6148
  43.6 199.7 %copy-start.15 = (f32[512,64]{0,1:T(8,128)}, f32[512,64]{0,1:T(8,128)S(1)}, u32[]{:S(2)}) copy-start(f32[512,64]{0,1:T(8,128)S(1)} %get-tuple-element.548) | copy-start | bytes 393220
  44.4 179.1 %all-gather.13.cloned.1.call-start = ((), (), s32[]{:S(2)}) async-start(), calls=%async_computation.8 | async-start | bytes 10485760 | tf_op jit(solution)/shard_map/all_gather | solution.py:189
  45.1 488.2 %all-gather.15.cloned.1.call-start = ((), (), s32[]{:S(2)}) async-start(), calls=%async_computation.9 | async-start | bytes 10485760 | tf_op jit(solution)/shard_map/all_gather | solution.py:191
  45.7 717.9 %all-gather.17.cloned.1.call-start = ((), (), s32[]{:S(2)}) async-start(), calls=%async_computation.10 | async-start | bytes 28835840 | tf_op jit(solution)/shard_map/all_gather | solution.py:231
  46.3 1108.2 %all-gather.21.cloned.1.call-start = ((), (), s32[]{:S(2)}) async-start(), calls=%async_computation.12 | async-start | bytes 28835840 | tf_op jit(solution)/shard_map/all_gather | solution.py:233
  46.9 1498.6 %all-gather.19.cloned.1.call-start = ((), (), s32[]{:S(2)}) async-start(), calls=%async_computation.11 | async-start | bytes 28835840 | tf_op jit(solution)/shard_map/all_gather | solution.py:232
  47.6 1987.9 %reduce-scatter.8.cloned.1.call-start = ((), (), s32[]{:S(2)}) async-start(), calls=%async_computation.13 | async-start | bytes 2359296 | tf_op jit(solution)/shard_map/reduce_scatter | solution.py:309
  546.5 608.0 %copy-start.9 = (bf16[1,512,2048]{2,1,0:T(8,128)(2,1)S(1)}, bf16[1,512,2048]{2,1,0:T(8,128)(2,1)}, u32[]{:S(2)}) copy-start(bf16[1,512,2048]{2,1,0:T(8,128)(2,1)} %param.20) | copy-start | bytes 6291460
  546.5 608.0 %copy-start.37 = (pred[512]{0:T(512)(128)(4,1)S(1)}, pred[512]{0:T(512)(128)(4,1)}, u32[]{:S(2)}) copy-start(pred[512]{0:T(512)(128)(4,1)} %get-tuple-element.526) | copy-start | bytes 1540
  1592.1 19.5 copy-start.7
  1699.1 17.9 slice-start
  1787.9 17.9 slice-start
  1832.3 17.9 slice-start
  1921.2 17.9 slice-start
  1991.4 44.1 copy-start.38
  1991.4 45.2 copy-start.33
  1991.4 45.2 copy-start.42
  1991.4 45.8 copy-start.3
  1991.4 45.8 copy-start.29
  1991.4 45.8 copy-start.35
  1995.8 372.3 %reduce-scatter.12.cloned.1.call-start = ((), (), s32[]{:S(2)}) async-start(), calls=%async_computation.15 | async-start | bytes 2162688 | tf_op jit(solution)/shard_map/reduce_scatter | solution.py:340
  2039.7 504.2 %reduce-scatter.14.cloned.1.call-start = ((), (), s32[]{:S(2)}) async-start(), calls=%async_computation.16 | async-start | bytes 17301504 | tf_op jit(solution)/shard_map/reduce_scatter | solution.py:343
  2053.0 856.0 %reduce-scatter.10.cloned.1.call-start = ((), (), s32[]{:S(2)}) async-start(), calls=%async_computation.14 | async-start | bytes 17301504 | tf_op jit(solution)/shard_map/reduce_scatter | solution.py:337
  2080.3 1801.7 %reduce-scatter.16.cloned.1.call-start = ((), (), s32[]{:S(2)}) async-start(), calls=%async_computation.17 | async-start | bytes 47579136 | tf_op jit(solution)/shard_map/reduce_scatter | solution.py:245
  2149.7 2708.0 %reduce-scatter.18.cloned.1.call-start = ((), (), s32[]{:S(2)}) async-start(), calls=%async_computation.18 | async-start | bytes 47579136 | tf_op jit(solution)/shard_map/reduce_scatter | solution.py:251
  2215.4 3617.9 %reduce-scatter.20.cloned.1.call-start = ((), (), s32[]{:S(2)}) async-start(), calls=%async_computation.19 | async-start | bytes 47579136 | tf_op jit(solution)/shard_map/reduce_scatter | solution.py:257
  (49 other events, 362.5 us)
Sparse Core Ops, SparseCore 0:
  9.6 30.6 all-gather.10
  44.5 27.6 all-gather.22
  73.8 149.6 all-gather.12
  224.9 147.8 all-gather.14
  374.3 389.3 all-gather.16
  765.1 389.3 all-gather.20
  1156.1 389.3 all-gather.18
  1995.9 39.5 reduce-scatter.7
  2039.8 138.2 reduce-scatter.11
  2180.8 363.0 reduce-scatter.13
  2546.8 362.1 reduce-scatter.9
  2911.7 970.2 reduce-scatter.15
  3884.9 972.7 reduce-scatter.17
  4860.5 972.7 reduce-scatter.19
where the time goes:
time: 5850 us; the launch traced here: 5840 us
  waiting for transfers between devices  4640 us (79%)
  matrix products  733 us (13%)
  local copies, waits for them, and re-layouts  224 us (4%)
  other arithmetic  138 us (2%)
  blocking collectives  68.2 us (1%)
    reduce_scatter x1, waiting for transfers between devices, shards(): lax.psum_scatter(split_term(normed_ffn, grad_up, ctx_count, fsdp_count),...  976 us
    reduce_scatter x1, waiting for transfers between devices, shards(): lax.psum_scatter(split_term(grad_out, hidden, ctx_count, fsdp_count), ('c...  976 us
    reduce_scatter x1, waiting for transfers between devices, shards(): lax.psum_scatter(split_term(normed_ffn, grad_gate, ctx_count, fsdp_count)...  973 us
    all_gather x1, waiting for transfers between devices, shards(): lax.all_gather(w_up, 'fsdp', axis=1, tiled=True)  373 us
    all_gather x1, waiting for transfers between devices, shards(): lax.all_gather(w_down, 'fsdp', axis=1, tiled=True)  371 us
    reduce_scatter x1, waiting for transfers between devices, shards(): lax.psum_scatter(contract_rows(normed_attn, grad_query), ('ctx', 'fsdp'),...  365 us
    dot_general x30, matrix products, contract_cols(): lax.dot_general(left, right, (((1,), (1,)), ((), ())), preferred_element_...  304 us
    all_gather x1, waiting for transfers between devices, shards(): lax.all_gather(w_gate, 'fsdp', axis=1, tiled=True)  217 us
  transfers between devices with their start and end apart: 14, of which 12 were waited for; matrix products, arithmetic and copies ran while one was open for 11% of the time, Pallas kernels for 0%

commit v1 on v0

--- a/solution.py
+++ b/solution.py
@@ -8,6 +8,28 @@
 EPSILON = 1e-05
 ROPE_BASE = 10000.0
 MASKED = -1e30
+
+
+def in_order(parts, dim):
+    dims = list(parts.shape[1:])
+    dims[dim] *= parts.shape[0]
+    return jnp.moveaxis(parts, 0, dim).reshape(dims)
+
+
+def gather_around(array, axis, dim):
+    count = lax.axis_size(axis)
+    pairs = [(i, (i + 1) % count) for i in range(count)]
+    back = [(b, a) for a, b in pairs]
+    lower, upper = ([], [])
+    for step in range(count - 1):
+        if step % 2 == 0:
+            lower.append(lax.ppermute(lower[-1] if lower else array, axis, pairs))
+        else:
+            upper.append(lax.ppermute(upper[-1] if upper else array, axis, back))
+    tiles = jnp.stack([*lower[::-1], array, *upper])
+    shift = lax.axis_index(axis) - len(lower)
+    tiles = tiles[(jnp.arange(count) - shift) % count]
+    return in_order(tiles, dim)
 
 
 def angles(positions, head_dim):
@@ -229,7 +251,7 @@
     )
     gate_full, up_full, down_full = (
         lax.all_gather(w_gate, "fsdp", axis=1, tiled=True),
-        lax.all_gather(w_up, "fsdp", axis=1, tiled=True),
+        gather_around(w_up, "fsdp", 1),
         lax.all_gather(w_down, "fsdp", axis=1, tiled=True),
     )
     gate_proj = jnp.dot(normed_ffn, gate_full, preferred_element_type=jnp.float32)

time: 5850 us -> 5790 us (0.990)
  waiting for transfers between devices: 4640 us -> 4020 us
  blocking collectives: 68.2 us -> 418 us
  local copies, waits for them, and re-layouts: 224 us -> 339 us
  starting transfers between devices: 1.13 us -> 108 us
    all_gather x1 -> x0, waiting for transfers between devices: 373 us -> none  [shards(): lax.all_gather(w_up, 'fsdp', axis=1, tiled=True)]
    all_gather x1, blocking collectives: 12.2 us -> 360 us  [shards(): lax.all_gather(gain_ffn, 'fsdp', axis=0, tiled=True)]
    all_gather x1, waiting for transfers between devices: 217 us -> 0.01 us  [shards(): lax.all_gather(w_gate, 'fsdp', axis=1, tiled=True)]
    ppermute x0 -> x3, waiting for transfers between devices: none -> 213 us  [the longest x2 213 us: gather_around(): lower.append(lax.ppermute(lower[-1] if lower else array, axis, pairs))]
    all_gather x1, waiting for transfers between devices: 148 us -> 0.01 us  [shards(): lax.all_gather(w_query, 'fsdp', axis=0, tiled=True)]
    ppermute x0 -> x3, starting transfers between devices: none -> 108 us  [the longest x2 106 us: gather_around(): lower.append(lax.ppermute(lower[-1] if lower else array, axis, pairs))]
    gather x0 -> x35, local copies, waits for them, and re-layouts: none -> 95.3 us
    all_gather x1, waiting for transfers between devices: 371 us -> 288 us  [shards(): lax.all_gather(w_down, 'fsdp', axis=1, tiled=True)]
  transfers between devices with their start and end apart: 14 -> 16, of which waited for: 12 -> 9; matrix products, arithmetic and copies ran while one was open for 11% -> 12% of each run, Pallas kernels for 0% -> 0%
where the time goes in v1:
time: 5790 us; the launch traced here: 5780 us
  waiting for transfers between devices  4020 us (69%)
  matrix products  710 us (12%)
  blocking collectives  418 us (7%)
  local copies, waits for them, and re-layouts  339 us (6%)
  other arithmetic  153 us (3%)
  starting transfers between devices  108 us (2%)
    reduce_scatter x1, waiting for transfers between devices, shards(): lax.psum_scatter(split_term(normed_ffn, grad_up, ctx_count, fsdp_count),...  976 us
    reduce_scatter x1, waiting for transfers between devices, shards(): lax.psum_scatter(split_term(normed_ffn, grad_gate, ctx_count, fsdp_count)...  976 us
    reduce_scatter x1, waiting for transfers between devices, shards(): lax.psum_scatter(split_term(grad_out, hidden, ctx_count, fsdp_count), ('c...  973 us
    reduce_scatter x1, waiting for transfers between devices, shards(): lax.psum_scatter(contract_rows(normed_attn, grad_query), ('ctx', 'fsdp'),...  365 us
    all_gather x1, blocking collectives, shards(): lax.all_gather(gain_ffn, 'fsdp', axis=0, tiled=True)  360 us
    all_gather x1, waiting for transfers between devices, shards(): lax.all_gather(w_down, 'fsdp', axis=1, tiled=True)  288 us
    dot_general x30, matrix products, contract_cols(): lax.dot_general(left, right, (((1,), (1,)), ((), ())), preferred_element_...  283 us
    ppermute x2, waiting for transfers between devices, gather_around(): lower.append(lax.ppermute(lower[-1] if lower else array, axis, pairs))  213 us
  transfers between devices with their start and end apart: 16, of which 9 were waited for; matrix products, arithmetic and copies ran while one was open for 12% of the time, Pallas kernels for 0%

profile of v1, /device:TPU:0, one launch (start us, length us, event | category | flops | bytes accessed | tf_op | source)
XLA Modules:
  0.0 5781.5 jit_solution(17441122073462700453)
XLA Ops:
  9.3 13.5 all-gather.1
  26.3 13.9 all-gather.10.cloned.1.call-done
  50.2 213.1 %collective-permute-done = bf16[2048,1408]{1,0:T(8,128)(2,1)} collective-permute-done((bf16[2048,1408]{1,0:T(8,128)(2,1)}, bf16[2048,1408]{1,0:T(8,128)(2,1)}, u32[]{:S(2)}, u32[]{:S(2)}) %collective-permute-start) | collective-permute-done | bytes 5767200 | tf_op jit(solution)/shard_map/ppermute | solution.py:26
  263.4 104.0 %collective-permute-start.1 = (bf16[2048,1408]{1,0:T(8,128)(2,1)}, bf16[2048,1408]{1,0:T(8,128)(2,1)}, u32[]{:S(2)}, u32[]{:S(2)}) collective-permute-start(bf16[2048,1408]{1,0:T(8,128)(2,1)} %collective-permute-done), channel_id=1, source_target_pairs={{0,1},{1,2},{2,3},{3,0},{4,5},{5,6},{6,7},{7,4},{8,9},{9,10},{10,1... | collective-permute-start | bytes 17301512 | tf_op jit(solution)/shard_map/ppermute | solution.py:26
  367.5 360.4 %all-gather.2 = bf16[4,1,512]{2,1,0:T(2,128)(2,1)S(1)} all-gather(bf16[1,1,512]{2,1,0:T(2,128)(2,1)S(1)} %reshape.479), channel_id=1, replica_groups=mesh['ctx'=8,'fsdp'=4] {'fsdp'}, dimensions={0}, use_global_device_ids=true | all-gather | bytes 5120 | tf_op jit(solution)/shard_map/all_gather | solution.py:215
  739.2 18.4 pad_maximum_fusion
  788.0 34.5 while.61
  826.5 34.5 while.60
  861.0 16.0 pad_maximum_fusion.1
  911.7 101.8 %while.62 = (s32[]{:T(128)}, f32[8192]{0:T(1024)S(1)}, f32[8192]{0:T(1024)S(1)}, s32[8]{0:T(128)S(1)}, s32[4096]{0:T(1024)S(1)}, /*index=5*/s32[]{:T(128)}, bf16...) while((s32[]{:T(128)}, f32[8192]{0:T(1024)S(1)}, ...), condition=%wide.region_4.5_spmd.clone, body=%wide.region_1.4_spmd.clone.sunk | while | flops 1111532032 | bytes 36384468 | solution.py:100
  1013.5 111.1 %while.63 = (s32[]{:T(128)}, f32[8192,128]{1,0:T(8,128)}, s32[8]{0:T(128)S(1)}, s32[4096]{0:T(1024)S(1)}, s32[]{:T(128)}, /*index=5*/bf16[4096,128]{1,0:T(8,128)...) while((s32[]{:T(128)}, f32[8192,128]{1,0:T(8,128)}, ...), condition=%wide.region_6.7_spmd.clone, body=%wide.region_5.6_spmd.clone.sunk | while | flops 2170552832 | bytes 10922712 | solution.py:116
  1146.4 20.1 fusion.105
  1166.5 287.9 %all-gather.18.cloned.1.call-done = bf16[2048,5632]{1,0:T(8,128)(2,1)} async-done(((bf16[2048,1408]{1,0:T(8,128)(2,1)}), bf16[2048,5632]{1,0:T(8,128)(2,1)}) %all-gather.18.cloned.1.call-update) | async-done | bytes 23068688 | tf_op jit(solution)/shard_map/all_gather | solution.py:255
  1454.3 18.4 convolution_convert_fusion
  1472.7 27.1 fusion.34
  1499.8 19.5 fusion.106
  1519.3 22.8 multiply_reduce_fusion
  1565.0 363.7 %while.64 = (s32[]{:T(128)}, f32[8192,128]{1,0:T(8,128)}, bf16[8,512,256]{1,2,0:T(8,128)(2,1)}, s32[8]{0:T(128)S(1)}, s32[4096]{0:T(1024)}, /*index=5*/s32[]{:T(...) while((s32[]{:T(128)}, f32[8192,128]{1,0:T(8,128)}, ...), condition=%wide.region_11.12_spmd.clone, body=%wide.region_10.11_spmd.clone.sunk | while | flops 5404885504 | bytes 160769360 | solution.py:153
  1937.4 39.5 reduce-scatter.8.cloned.1.call-done
  2039.1 20.8 convolution_bitcast_fusion
  2059.9 33.4 copy.107
  2108.6 21.0 convolution_bitcast_fusion.2
  2129.5 33.4 copy.101
  2174.3 21.0 convolution_bitcast_fusion.1
  2195.2 33.5 copy.104
  2229.4 19.9 fusion.59
  2261.3 43.8 all-reduce.2
  2312.2 173.1 %reduce-scatter.14.cloned.1.call-done = f32[64,2048]{1,0:T(8,128)} async-done(((f32[2048,2048]{1,0:T(8,128)}), f32[64,2048]{1,0:T(8,128)}) %reduce-scatter.14.cloned.1.call-update) | async-done | bytes 524304 | tf_op jit(solution)/shard_map/reduce_scatter | solution.py:365
  2485.4 364.9 %reduce-scatter.10.cloned.1.call-done = f32[64,2048]{1,0:T(8,128)} async-done(((f32[2048,2048]{1,0:T(8,128)}), f32[64,2048]{1,0:T(8,128)}) %reduce-scatter.10.cloned.1.call-update) | async-done | bytes 524304 | tf_op jit(solution)/shard_map/reduce_scatter | solution.py:359
  2850.3 973.2 %reduce-scatter.20.cloned.1.call-done = f32[256,1408]{1,0:T(8,128)} async-done(((f32[8192,1408]{1,0:T(8,128)}), f32[256,1408]{1,0:T(8,128)}) %reduce-scatter.20.cloned.1.call-update) | async-done | bytes 1441808 | tf_op jit(solution)/shard_map/reduce_scatter | solution.py:279
  3823.5 975.5 %reduce-scatter.16.cloned.1.call-done = f32[256,1408]{1,0:T(8,128)} async-done(((f32[8192,1408]{1,0:T(8,128)}), f32[256,1408]{1,0:T(8,128)}) %reduce-scatter.16.cloned.1.call-update) | async-done | bytes 1441808 | tf_op jit(solution)/shard_map/reduce_scatter | solution.py:267
  4799.0 975.7 %reduce-scatter.18.cloned.1.call-done = f32[256,1408]{1,0:T(8,128)} async-done(((f32[8192,1408]{1,0:T(8,128)}), f32[256,1408]{1,0:T(8,128)}) %reduce-scatter.18.cloned.1.call-update) | async-done | bytes 1441808 | tf_op jit(solution)/shard_map/reduce_scatter | solution.py:273
  (485 shorter events, 884.4 us)
Async XLA Ops:
  7.2 33.1 all-gather.10.cloned.1.call-start
  7.9 720.7 %all-gather.20.cloned.1.call-start = ((), (), s32[]{:S(2)}) async-start(), calls=%async_computation.19 | async-start | bytes 2359296 | tf_op jit(solution)/shard_map/all_gather | solution.py:231
  22.8 866.3 %copy-start.30 = (f32[4,1,512]{2,1,0:T(1,128)}, f32[4,1,512]{2,1,0:T(1,128)S(1)}, u32[]{:S(2)}) copy-start(f32[4,1,512]{2,1,0:T(1,128)S(1)} %convert_element_type.188) | copy-start | bytes 24580
  24.2 20.1 copy-start.35
  24.2 20.1 copy-start.44
  26.3 862.8 %copy-start.37 = (f32[512]{0:T(512)}, f32[512]{0:T(512)S(1)}, u32[]{:S(2)}) copy-start(f32[512]{0:T(512)S(1)} %add_rsqrt_fusion.1) | copy-start | bytes 6148
  43.6 852.7 %copy-start.16 = (f32[512,64]{0,1:T(8,128)}, f32[512,64]{0,1:T(8,128)S(1)}, u32[]{:S(2)}) copy-start(f32[512,64]{0,1:T(8,128)S(1)} %get-tuple-element.614) | copy-start | bytes 393220
  44.4 832.5 %all-gather.12.cloned.1.call-start = ((), (), s32[]{:S(2)}) async-start(), calls=%async_computation.8 | async-start | bytes 10485760 | tf_op jit(solution)/shard_map/all_gather | solution.py:211
  45.1 1088.1 %all-gather.14.cloned.1.call-start = ((), (), s32[]{:S(2)}) async-start(), calls=%async_computation.9 | async-start | bytes 10485760 | tf_op jit(solution)/shard_map/all_gather | solution.py:213
  45.7 1100.7 %all-gather.16.cloned.1.call-start = ((), (), s32[]{:S(2)}) async-start(), calls=%async_computation.10 | async-start | bytes 28835840 | tf_op jit(solution)/shard_map/all_gather | solution.py:253
  46.3 321.2 %copy-start.46 = (bf16[512]{0:T(512)(128)(2,1)S(1)}, bf16[512]{0:T(512)(128)(2,1)}, u32[]{:S(2)}) copy-start(bf16[512]{0:T(512)(128)(2,1)} %param.28) | copy-start | bytes 3076
  46.3 1408.0 %all-gather.18.cloned.1.call-start = ((), (), s32[]{:S(2)}) async-start(), calls=%async_computation.11 | async-start | bytes 28835840 | tf_op jit(solution)/shard_map/all_gather | solution.py:255
  46.4 217.0 %collective-permute-start = (bf16[2048,1408]{1,0:T(8,128)(2,1)}, bf16[2048,1408]{1,0:T(8,128)(2,1)}, u32[]{:S(2)}, u32[]{:S(2)}) collective-permute-start(bf16[2048,1408]{1,0:T(8,128)(2,1)} %param.30), channel_id=1, source_target_pairs={{0,1},{1,2},{2,3},{3,0},{4,5},{5,6},{6,7},{7,4},{8,9},{9,10},{10,1... | collective-permute-start | bytes 17301512 | tf_op jit(solution)/shard_map/ppermute | solution.py:26
  47.9 685.1 %collective-permute-start.2 = (bf16[2048,1408]{1,0:T(8,128)(2,1)}, bf16[2048,1408]{1,0:T(8,128)(2,1)}, u32[]{:S(2)}, u32[]{:S(2)}) collective-permute-start(bf16[2048,1408]{1,0:T(8,128)(2,1)} %param.30), channel_id=1, source_target_pairs={{1,0},{2,1},{3,2},{0,3},{5,4},{6,5},{7,6},{4,7},{9,8},{10,9},{11,1... | collective-permute-start | bytes 17301512 | tf_op jit(solution)/shard_map/ppermute | solution.py:28
  263.4 469.6 %collective-permute-start.1 = (bf16[2048,1408]{1,0:T(8,128)(2,1)}, bf16[2048,1408]{1,0:T(8,128)(2,1)}, u32[]{:S(2)}, u32[]{:S(2)}) collective-permute-start(bf16[2048,1408]{1,0:T(8,128)(2,1)} %collective-permute-done), channel_id=1, source_target_pairs={{0,1},{1,2},{2,3},{3,0},{4,5},{5,6},{6,7},{7,4},{8,9},{9,10},{10,1... | collective-permute-start | bytes 17301512 | tf_op jit(solution)/shard_map/ppermute | solution.py:26
  367.4 1609.5 %reduce-scatter.8.cloned.1.call-start = ((), (), s32[]{:S(2)}) async-start(), calls=%async_computation.12 | async-start | bytes 2359296 | tf_op jit(solution)/shard_map/reduce_scatter | solution.py:331
  1146.4 307.9 %copy-start.11 = (bf16[1,512,2048]{2,1,0:T(8,128)(2,1)S(1)}, bf16[1,512,2048]{2,1,0:T(8,128)(2,1)}, u32[]{:S(2)}) copy-start(bf16[1,512,2048]{2,1,0:T(8,128)(2,1)} %param.20) | copy-start | bytes 6291460
  1146.4 307.9 %copy-start.40 = (pred[512]{0:T(512)(128)(4,1)S(1)}, pred[512]{0:T(512)(128)(4,1)}, u32[]{:S(2)}) copy-start(pred[512]{0:T(512)(128)(4,1)} %get-tuple-element.590) | copy-start | bytes 1540
  1519.3 22.8 copy-start.9
  1587.3 16.6 copy-start.1
  1932.8 44.1 copy-start.41
  1932.8 45.2 copy-start.36
  1932.8 45.2 copy-start.45
  1932.8 45.8 copy-start.5
  1932.8 45.8 copy-start.31
  1932.8 45.8 copy-start.38
  1937.2 375.0 %reduce-scatter.12.cloned.1.call-start = ((), (), s32[]{:S(2)}) async-start(), calls=%async_computation.14 | async-start | bytes 2162688 | tf_op jit(solution)/shard_map/reduce_scatter | solution.py:362
  1981.0 504.3 %reduce-scatter.14.cloned.1.call-start = ((), (), s32[]{:S(2)}) async-start(), calls=%async_computation.15 | async-start | bytes 17301504 | tf_op jit(solution)/shard_map/reduce_scatter | solution.py:365
  1994.3 856.0 %reduce-scatter.10.cloned.1.call-start = ((), (), s32[]{:S(2)}) async-start(), calls=%async_computation.13 | async-start | bytes 17301504 | tf_op jit(solution)/shard_map/reduce_scatter | solution.py:359
  2022.1 1801.4 %reduce-scatter.20.cloned.1.call-start = ((), (), s32[]{:S(2)}) async-start(), calls=%async_computation.18 | async-start | bytes 47579136 | tf_op jit(solution)/shard_map/reduce_scatter | solution.py:279
  2093.3 2705.8 %reduce-scatter.16.cloned.1.call-start = ((), (), s32[]{:S(2)}) async-start(), calls=%async_computation.16 | async-start | bytes 47579136 | tf_op jit(solution)/shard_map/reduce_scatter | solution.py:267
  2162.9 3611.8 %reduce-scatter.18.cloned.1.call-start = ((), (), s32[]{:S(2)}) async-start(), calls=%async_computation.17 | async-start | bytes 47579136 | tf_op jit(solution)/shard_map/reduce_scatter | solution.py:273
  (54 other events, 357.7 us)
Sparse Core Ops, SparseCore 0:
  9.6 30.6 all-gather.9
  44.5 27.6 all-gather.19
  73.8 303.2 all-gather.11
  378.5 282.0 all-gather.13
  662.1 400.7 all-gather.15
  1064.4 389.9 all-gather.17
  1937.3 39.4 reduce-scatter.7
  1981.2 138.2 reduce-scatter.11
  2122.4 362.9 reduce-scatter.13
  2488.1 362.1 reduce-scatter.9
  2853.2 970.2 reduce-scatter.19
  3826.2 972.7 reduce-scatter.15
  4801.9 972.7 reduce-scatter.17
